TPU v7x, 32 devices: a whole 2x2x4 slice. The times are simulated.
32 devices in a mesh: reach: 2 (over y), row: 4 (over z), col: 4 (over x, core).
Axes of the slice: x: 2, y: 2, z: 4, core: 2. Of those that a mesh axis runs over, the one named last changes fastest.
Arguments:
- operator: float32 [2048, 65536], P(('reach', 'col'), 'row'), parts along dimension 0, may hold values from -0.03125 to 0.03125
- basis: float32 [131072, 256], P(('reach', 'row')), parts along dimension 0, may hold values from -6 to 6
Outputs:
- image: float32 [2048, 256], P(('reach', 'row')), parts along dimension 0
There are 2 independent parts, one for each index of `reach`. A program takes and returns all parts, laid end to end along the dimension named above; each array names one. Nothing has to cross between parts.
All inputs are finite; a program needn't handle non-finite values.
Results may differ from a plain program's by a relative error of at most 0.000071.
Values sent between devices are 32-bit elements; how exact they have to be, the bound alone decides.
No kernel may reach another device: no remote copies, remote signals or barrier semaphores. Data moves between devices by JAX's collectives and lax.ppermute only.
A program may use at most 64 MiB of HBM per device.

v0:
```python
import jax
import jax.numpy as jnp
from jax import lax
from jax.sharding import PartitionSpec as P


def spread(value, axis, source):
    kept = jnp.where(lax.axis_index(axis) == source, value, 0).astype(value.dtype)
    return lax.psum(kept, axis)


def shards(operator, basis):
    partial_sum = jnp.dot(
        operator, basis, preferred_element_type=jnp.float32, precision=lax.Precision.HIGHEST
    )
    tile_rows = operator.shape[0]
    n_row = lax.axis_size("row")
    n_col = lax.axis_size("col")
    group = n_row // n_col
    out_rows = tile_rows * n_col // n_row
    summed = lax.psum(partial_sum, "row")
    row_index = lax.axis_index("row")
    offset = row_index % group * out_rows
    picked = lax.dynamic_slice_in_dim(summed, offset, out_rows, 0)
    return spread(picked, "col", row_index // group)


def solution(mesh):
    in_specs = (P(("reach", "col"), "row"), P(("reach", "row"), None))
    out_specs = P(("reach", "row"), None)
    return jax.shard_map(shards, mesh=mesh, in_specs=in_specs, out_specs=out_specs, check_vma=False)
```

profile of v0, /device:TPU:0, one launch (start us, length us, event | category | flops | bytes accessed | tf_op | source)
XLA Modules:
  0.0 106.0 jit_solution(11191584294463896214)
XLA Ops:
  6.5 0.0 all-reduce.3.cloned.1.call-start
  6.5 18.6 %fusion = f32[256,256]{1,0:T(8,128)} fusion(f32[256,16384]{1,0:T(8,128)} %param.2, f32[16384,256]{1,0:T(8,128)} %param.3), kind=kOutput, calls=%fused_computation.1 | convolution fusion | flops 12884901888 | bytes 33816576 | tf_op jit(solution)/shard_map/dot_general | solution.py:13
  25.2 0.0 all-reduce.3.cloned.1.call-update
  25.2 0.0 all-reduce.5.cloned.1.call-start
  25.2 38.1 %all-reduce.3.cloned.1.call-done = f32[256,256]{1,0:T(8,128)} async-done(((f32[256,256]{1,0:T(8,128)}), f32[256,256]{1,0:T(8,128)}) %all-reduce.3.cloned.1.call-update) | async-done | bytes 262160 | tf_op jit(solution)/shard_map/psum | solution.py:21
  63.3 1.7 %broadcast_select_fusion = f32[256,256]{1,0:T(8,128)} fusion(f32[256,256]{1,0:T(8,128)} %all-reduce.3.cloned.1.call-done, pred[]{:T(512)S(6)} %eq.5), kind=kLoop, calls=%fused_computation | loop fusion | flops 65536 | bytes 524289 | tf_op jit(solution)/shard_map/jit(_where)/select_n | solution.py:8
  65.0 0.0 all-reduce.5.cloned.1.call-update
  65.0 32.5 %all-reduce.5.cloned.1.call-done = f32[256,256]{1,0:T(8,128)} async-done(((f32[256,256]{1,0:T(8,128)}), f32[256,256]{1,0:T(8,128)}) %all-reduce.5.cloned.1.call-update) | async-done | bytes 262160 | tf_op jit(solution)/shard_map/psum | solution.py:9
  97.5 1.7 %copy.5 = f32[256,256]{1,0:T(8,128)} copy(f32[256,256]{1,0:T(8,128)} %all-reduce.5.cloned.1.call-done) | data formatting | bytes 524288
Async XLA Ops:
  6.5 56.8 %all-reduce.3.cloned.1.call-start = ((), (), s32[]{:S(2)}) async-start(), calls=%async_computation | async-start | bytes 524288 | tf_op jit(solution)/shard_map/psum | solution.py:21
  25.2 72.3 %all-reduce.5.cloned.1.call-start = ((), (), s32[]{:S(2)}) async-start(), calls=%async_computation.1 | async-start | bytes 524288 | tf_op jit(solution)/shard_map/psum | solution.py:9
Sparse Core Ops, SparseCore 0:
  25.3 37.9 all-reduce.2
  65.8 31.6 all-reduce.4
where the time goes:
time: 106 us
  waiting for transfers between devices  70.6 us (67%)
  matrix products  18.6 us (18%)
  between operations  13.4 us (13%)
  other arithmetic  1.67 us (2%)
  local copies, waits for them, and re-layouts  1.67 us (2%)
    psum x1, waiting for transfers between devices, shards(): summed = lax.psum(partial_sum, 'row')  38.1 us
    psum x1, waiting for transfers between devices, spread(): return lax.psum(kept, axis)  32.5 us
    dot_general x1, matrix products, shards(): jnp.dot(operator, basis, preferred_element_type=jnp.float32, precision=la...  18.6 us
  transfers between devices with their start and end apart: 2, of which 2 were waited for; matrix products, arithmetic and copies ran while one was open for 0% of the time, Pallas kernels for 0%

commit v1 on v0

--- a/solution.py
+++ b/solution.py
@@ -18,7 +18,7 @@
     n_col = lax.axis_size("col")
     group = n_row // n_col
     out_rows = tile_rows * n_col // n_row
-    summed = lax.psum(partial_sum, "row")
+    summed = jnp.sum(lax.all_gather(partial_sum, "row"), axis=0)
     row_index = lax.axis_index("row")
     offset = row_index % group * out_rows
     picked = lax.dynamic_slice_in_dim(summed, offset, out_rows, 0)

time: 106 us -> 98.5 us (0.929)
  waiting for transfers between devices: 70.6 us -> 62.5 us
    psum x1 -> x0, waiting for transfers between devices: 38.1 us -> none  [shards(): summed = lax.psum(partial_sum, 'row')]
    all_gather x0 -> x1, waiting for transfers between devices: none -> 30.7 us  [shards(): summed = jnp.sum(lax.all_gather(partial_sum, 'row'), axis=0)]
    reduce_sum x0 -> x1, other arithmetic: none -> 1.32 us  [shards(): summed = jnp.sum(lax.all_gather(partial_sum, 'row'), axis=0)]
where the time goes in v1:
time: 98.5 us; the launch traced here: 98.3 us
  waiting for transfers between devices  62.5 us (63%)
  matrix products  18.6 us (19%)
  between operations  13.4 us (14%)
  other arithmetic  2.05 us (2%)
  local copies, waits for them, and re-layouts  1.67 us (2%)
    psum x1, waiting for transfers between devices, spread(): return lax.psum(kept, axis)  31.8 us
    all_gather x1, waiting for transfers between devices, shards(): summed = jnp.sum(lax.all_gather(partial_sum, 'row'), axis=0)  30.7 us
    dot_general x1, matrix products, shards(): jnp.dot(operator, basis, preferred_element_type=jnp.float32, precision=la...  18.6 us
  transfers between devices with their start and end apart: 2, of which 2 were waited for; matrix products, arithmetic and copies ran while one was open for 0% of the time, Pallas kernels for 0%

profile of v1, /device:TPU:0, one launch (start us, length us, event | category | flops | bytes accessed | tf_op | source)
XLA Modules:
  0.0 98.3 jit_solution(8070072653539677769)
XLA Ops:
  6.5 0.0 all-gather.3.cloned.1.call-start
  6.5 18.6 %fusion = f32[256,256]{1,0:T(8,128)} fusion(f32[256,16384]{1,0:T(8,128)} %param.2, f32[16384,256]{1,0:T(8,128)} %param.3), kind=kOutput, calls=%fused_computation.1 | convolution fusion | flops 12884901888 | bytes 33816576 | tf_op jit(solution)/shard_map/dot_general | solution.py:13
  25.2 0.0 all-gather.3.cloned.1.call-update
  25.2 0.0 all-reduce.2.cloned.1.call-start
  25.2 30.7 %all-gather.3.cloned.1.call-done = f32[1024,256]{1,0:T(8,128)} async-done(((f32[256,256]{1,0:T(8,128)}), f32[1024,256]{1,0:T(8,128)}) %all-gather.3.cloned.1.call-update) | async-done | bytes 1048592 | tf_op jit(solution)/shard_map/all_gather | solution.py:21
  56.0 1.3 %reduce_sum.9 = f32[256,256]{1,0:T(8,128)S(1)} reduce(f32[4,256,256]{2,1,0:T(8,128)} %bitcast.3, f32[]{:T(128)} %constant.29.clone.1), dimensions={0}, to_apply=%region_0.0 | reduce | flops 196608 | bytes 1310724 | tf_op jit(solution)/shard_map/reduce_sum | solution.py:21
  57.3 0.7 broadcast_select_fusion
  58.0 0.0 all-reduce.2.cloned.1.call-update
  58.0 31.8 %all-reduce.2.cloned.1.call-done = f32[256,256]{1,0:T(8,128)} async-done(((f32[256,256]{1,0:T(8,128)}), f32[256,256]{1,0:T(8,128)}) %all-reduce.2.cloned.1.call-update) | async-done | bytes 262160 | tf_op jit(solution)/shard_map/psum | solution.py:9
  89.8 1.7 %copy.4 = f32[256,256]{1,0:T(8,128)} copy(f32[256,256]{1,0:T(8,128)} %all-reduce.2.cloned.1.call-done) | data formatting | bytes 524288
Async XLA Ops:
  6.5 49.4 %all-gather.3.cloned.1.call-start = ((), (), s32[]{:S(2)}) async-start(), calls=%async_computation.1 | async-start | bytes 1310720 | tf_op jit(solution)/shard_map/all_gather | solution.py:21
  25.2 64.6 %all-reduce.2.cloned.1.call-start = ((), (), s32[]{:S(2)}) async-start(), calls=%async_computation | async-start | bytes 524288 | tf_op jit(solution)/shard_map/psum | solution.py:9
Sparse Core Ops, SparseCore 0:
  25.3 30.6 all-gather.2
  58.3 31.4 all-reduce.1
